TPU v7x, 32 devices: a whole 2x2x4 slice. The times are simulated.
32 devices in a mesh: dp: 8 (over y, x, core), seq: 4 (over z).
Axes of the slice: x: 2, y: 2, z: 4, core: 2. Of those that a mesh axis runs over, the one named last changes fastest.
Arguments:
- tokens: bfloat16 [8, 2048, 768], P('dp', 'seq'), may hold values from -6 to 6
- cotangent: bfloat16 [8, 2048, 768], P('dp', 'seq'), may hold values from -6 to 6
- segment_ids: int32 [8, 2048], P('dp', 'seq'), may hold values from 0 to 7, as said below
- doc_starts: int32 [8, 2048], P('dp', 'seq'), may hold values from 0 to 1, as said below
- valid_mask: int32 [8, 2048], P('dp', 'seq'), may hold values from 0 to 1
- step_number: int32 [1], replicated, may hold values from 1 to 64
- learn_rate: float32 [1], replicated, may hold values from 0.001 to 0.004
- norm_gain: float32 [768], replicated, may hold values from 0.5 to 1.5
- in_weight: bfloat16 [768, 3352], replicated, may hold values from -0.21875 to 0.21875
- conv_weight: float32 [4, 1792], replicated, may hold values from -3 to 3
- conv_bias: float32 [1792], replicated, may hold values from -1.75 to 1.75
- dt_bias: float32 [24], replicated, may hold values from -6 to -2
- a_log: float32 [24], replicated, may hold values from -1 to 2.5
- skip_d: float32 [24], replicated, may hold values from 0.5 to 1.5
- gate_gain: float32 [1536], replicated, may hold values from 0.5 to 1.5
- out_weight: bfloat16 [1536, 768], replicated, may hold values from -0.15625 to 0.15625
- in_momentum: float32 [768, 3352], P('seq'), may hold values from -6 to 6
- out_momentum: float32 [1536, 768], P(None, 'seq'), may hold values from -448 to 448
Outputs:
- output: bfloat16 [8, 2048, 768], P('dp', 'seq')
- input_grad: bfloat16 [8, 2048, 768], P('dp', 'seq')
- new_in_weight: bfloat16 [768, 3352], replicated
- new_out_weight: bfloat16 [1536, 768], replicated
- new_in_momentum: float32 [768, 3352], P('seq')
- new_out_momentum: float32 [1536, 768], P(None, 'seq')
- norm_gain_grad: float32 [768], replicated
- conv_weight_grad: float32 [4, 1792], replicated
- conv_bias_grad: float32 [1792], replicated
- dt_bias_grad: float32 [24], replicated
- a_log_grad: float32 [24], replicated
- skip_grad: float32 [24], replicated
- gate_gain_grad: float32 [1536], replicated
- output_rms: float32 [1], replicated
- mixer_rms: float32 [1], replicated
Inputs may be any that keep to these rules, and one draw needn't show every extreme that they name: Within each sequence segment_ids never fall, are 0 at the first position and rise by one exactly where doc_starts is 1; every sequence holds exactly 8 documents. `doc_starts`: 1 at the first position of every sequence; exactly 8 ones in every sequence.
All inputs are finite; a program needn't handle non-finite values.
Results may differ from a plain program's by a relative error of at most 0.0066.
The roundings to bfloat16 on the way count: a program that leaves them out, or rounds other values in their place, can miss the bound.
Values may be sent and summed in bfloat16 or wider, within the bound.
A program may use at most 192 MiB of HBM per device.

v0:
```python
import jax
import jax.numpy as jnp
from jax import lax
from jax.sharding import PartitionSpec as P

epsilon = 1e-05
highest = lax.Precision.HIGHEST


def shifted(block, axis, distance):
    devices = range(lax.axis_size(axis))
    route = [(i - distance, i) for i in devices if i - distance in devices]
    return lax.ppermute(block, axis, route)


def entering(value, axis, join, neutral):
    place = lax.axis_index(axis)
    gathered = jax.tree.map(
        lambda a, kind: lax.all_gather(a.astype(kind), axis), value, (jnp.bfloat16, jnp.bfloat16)
    )
    state = jax.tree.map(lambda a, e: jnp.zeros_like(a) + jnp.asarray(e, a.dtype), value, neutral)

    def one(step, state):
        return join(
            state,
            jax.tree.map(
                lambda a, own: lax.dynamic_index_in_dim(a, step, 0, False).astype(own.dtype),
                gathered,
                value,
            ),
        )

    return lax.fori_loop(0, place, one, state)


def carried_in(value, axis, combine, identity):
    length, mine = (lax.axis_size(axis), lax.axis_index(axis))
    everything = jax.tree.map(lambda part: lax.all_gather(part, axis), value)
    start = jax.tree.map(
        lambda part, zero: jnp.broadcast_to(jnp.asarray(zero, part.dtype), part.shape),
        value,
        identity,
    )

    def step(k, before):
        at = length - 1 - k
        reached = at > mine
        new = combine(before, jax.tree.map(lambda part: part[at], everything))
        return jax.tree.map(lambda a, b: jnp.where(reached, a, b), new, before)

    return lax.fori_loop(0, length, step, start)


def pre_norm(values, gain_values):
    return (
        values
        * lax.rsqrt(jnp.mean(values * values, axis=-1, keepdims=True) + epsilon)
        * gain_values
    )


def compose(earlier, later):
    return (earlier[0] * later[0], later[0][:, :, None, None] * earlier[1] + later[1])


def local(
    tokens,
    cotangent,
    segment_ids,
    doc_starts,
    valid_mask,
    step_number,
    learn_rate,
    norm_gain,
    in_weight,
    conv_weight,
    conv_bias,
    dt_bias,
    a_log,
    skip_d,
    gate_gain,
    out_weight,
    in_momentum,
    out_momentum,
):
    seq_count, piece_size, model_width = tokens.shape
    head_count = dt_bias.shape[0]
    tap_count, channels = conv_weight.shape
    inner_width = gate_gain.shape[0]
    state_width = (channels - inner_width) // 2
    head_width = inner_width // head_count
    proj_width = in_weight.shape[1]
    row_count = seq_count * piece_size
    inputs = tokens.astype(jnp.float32)
    normed_in, back_pre = jax.vjp(pre_norm, inputs, norm_gain)
    normed_low = normed_in.astype(jnp.bfloat16).reshape(row_count, model_width)
    projected = jnp.dot(normed_low, in_weight, preferred_element_type=jnp.float32).reshape(
        seq_count, piece_size, proj_width
    )
    gate_in = projected[:, :, :inner_width]
    conv_in = projected[:, :, inner_width : inner_width + channels]
    dt_raw = projected[:, :, inner_width + channels :]
    seg_float = segment_ids.astype(jnp.float32)
    prev_rows, prev_seg = shifted(
        (conv_in[:, piece_size - tap_count + 1 :], seg_float[:, piece_size - tap_count + 1 :]),
        "seq",
        1,
    )
    padded = jnp.concatenate([prev_rows, conv_in], axis=1)
    seg_pad = jnp.concatenate([prev_seg, seg_float], axis=1)
    masks = [
        (seg_pad[:, k : k + piece_size] == seg_float).astype(jnp.float32)[:, :, None]
        for k in range(tap_count)
    ]

    def conv_part(padded_in, taps_in, bias_in, raw_in, dt_bias_in, a_log_in):
        summed = bias_in + jnp.zeros((seq_count, piece_size, channels), jnp.float32)
        for k in range(tap_count):
            summed = summed + padded_in[:, k : k + piece_size] * masks[k] * taps_in[k]
        activated = jax.nn.silu(summed)
        signal = activated[:, :, :inner_width].reshape(
            seq_count, piece_size, head_count, head_width
        )
        writer = activated[:, :, inner_width : inner_width + state_width]
        reader = activated[:, :, inner_width + state_width :]
        step_size = jax.nn.softplus(raw_in + dt_bias_in)
        return (signal, writer, reader, step_size, -jnp.exp(a_log_in) * step_size)

    (signal, writer, reader, step_size, log_decay), back_conv = jax.vjp(
        conv_part, padded, conv_weight, conv_bias, dt_raw, dt_bias, a_log
    )
    counter = jnp.cumsum(doc_starts, axis=1)
    positions = jnp.arange(piece_size)
    causal = positions[:, None] >= positions[None, :]
    same_doc = (counter[:, :, None] == counter[:, None, :]) & causal[None]
    first_doc = (counter == 0)[:, :, None]
    last_doc = (counter == counter[:, -1:])[:, :, None]
    untouched = (counter[:, -1] == 0)[:, None]

    def end_state(signal_in, writer_in, step_in, decay_in):
        cumulative = jnp.cumsum(decay_in, axis=1)
        final_log = cumulative[:, -1]
        keeping = jnp.where(untouched, jnp.exp(final_log), 0.0)
        tails = jnp.where(last_doc, jnp.exp(final_log[:, None] - cumulative), 0.0) * step_in
        fresh_state = jnp.einsum(
            "slh,slhp,sln->shpn", tails, signal_in, writer_in, precision=highest
        )
        return (keeping, fresh_state)

    def piece_out(signal_in, writer_in, reader_in, step_in, decay_in, incoming_in):
        cumulative = jnp.cumsum(decay_in, axis=1)
        by_head = jnp.transpose(cumulative, (0, 2, 1))
        gaps = by_head[:, :, :, None] - by_head[:, :, None, :]
        decays = jnp.exp(jnp.where(same_doc[:, None], gaps, -1e30))
        scores = jnp.einsum("stn,sun->stu", reader_in, writer_in, precision=highest)
        weighted = scores[:, None] * decays
        inner_part = jnp.einsum(
            "shtu,suhp->sthp", weighted, signal_in * step_in[..., None], precision=highest
        )
        entries = jnp.where(first_doc, jnp.exp(cumulative), 0.0)
        carried = (
            jnp.einsum("stn,shpn->sthp", reader_in, incoming_in, precision=highest)
            * entries[..., None]
        )
        return inner_part + carried

    (keeping, fresh_state), back_end = jax.vjp(end_state, signal, writer, step_size, log_decay)
    identity = (jnp.ones_like(keeping), jnp.zeros_like(fresh_state))
    _, incoming = entering((keeping, fresh_state), "seq", compose, identity)
    ssm_out, back_out = jax.vjp(piece_out, signal, writer, reader, step_size, log_decay, incoming)

    def gate_norm(ssm_in, signal_in, skip_in, gate_values, gain_values):
        mixer_in = (ssm_in + skip_in[:, None] * signal_in).reshape(
            seq_count, piece_size, inner_width
        )
        gated_out = mixer_in * jax.nn.silu(gate_values)
        return (
            gated_out
            * lax.rsqrt(jnp.mean(gated_out * gated_out, axis=-1, keepdims=True) + epsilon)
            * gain_values
        )

    gate_normed, back_gate = jax.vjp(gate_norm, ssm_out, signal, skip_d, gate_in, gate_gain)
    gate_low = gate_normed.astype(jnp.bfloat16).reshape(row_count, inner_width)
    mixed = jnp.dot(gate_low, out_weight, preferred_element_type=jnp.float32).reshape(
        seq_count, piece_size, model_width
    )
    block_out = inputs + mixed
    valid_float = valid_mask.astype(jnp.float32)
    out_square = jnp.sum(valid_float * jnp.sum(block_out * block_out, axis=-1))
    mix_square = jnp.sum(valid_float * jnp.sum(mixed * mixed, axis=-1))
    valid_count = jnp.sum(valid_float)
    out_grad = cotangent.astype(jnp.float32) * valid_float[:, :, None]
    out_low = out_grad.astype(jnp.bfloat16).reshape(row_count, model_width)
    gate_grad = lax.dot_general(
        out_low, out_weight, (((1,), (1,)), ((), ())), preferred_element_type=jnp.float32
    ).reshape(seq_count, piece_size, inner_width)
    ssm_grad, signal_grad_gate, skip_grad, gate_in_grad, gate_gain_grad = back_gate(gate_grad)
    signal_grad_out, writer_grad_out, reader_grad, step_grad_out, decay_grad_out, state_grad = (
        back_out(ssm_grad)
    )
    _, later_grad = carried_in((keeping, state_grad), "seq", compose, identity)
    keeping_grad = jnp.sum(later_grad * incoming, axis=(2, 3))
    signal_grad_end, writer_grad_end, step_grad_end, decay_grad_end = back_end(
        (keeping_grad, later_grad)
    )
    padded_grad, conv_weight_grad, conv_bias_grad, dt_raw_grad, dt_bias_grad, a_log_grad = (
        back_conv(
            (
                signal_grad_gate + signal_grad_out + signal_grad_end,
                writer_grad_out + writer_grad_end,
                reader_grad,
                step_grad_out + step_grad_end,
                decay_grad_out + decay_grad_end,
            )
        )
    )
    rim_grad = shifted(padded_grad[:, : tap_count - 1].astype(jnp.bfloat16), "seq", -1).astype(
        jnp.float32
    )
    conv_in_grad = padded_grad[:, tap_count - 1 :] + jnp.pad(
        rim_grad, ((0, 0), (piece_size - tap_count + 1, 0), (0, 0))
    )
    proj_grad = (
        jnp.concatenate([gate_in_grad, conv_in_grad, dt_raw_grad], axis=2)
        .astype(jnp.bfloat16)
        .reshape(row_count, proj_width)
    )
    normed_grad = lax.dot_general(
        proj_grad, in_weight, (((1,), (1,)), ((), ())), preferred_element_type=jnp.float32
    ).reshape(seq_count, piece_size, model_width)
    input_grad_pre, norm_gain_grad = back_pre(normed_grad)
    input_grad = (out_grad + input_grad_pre).astype(jnp.bfloat16)
    share_rows = model_width // lax.axis_size("seq")
    in_part = lax.dot_general(
        normed_low, proj_grad, (((0,), (0,)), ((), ())), preferred_element_type=jnp.float32
    )
    out_part = lax.dot_general(
        out_low, gate_low, (((0,), (0,)), ((), ())), preferred_element_type=jnp.float32
    )
    whole_grad = lax.psum(jnp.concatenate([in_part, out_part], axis=1), "dp")
    grad_share = lax.psum_scatter(whole_grad, "seq", scatter_dimension=0, tiled=True)
    step_float = step_number[0].astype(jnp.float32)
    rate_now = learn_rate[0] * step_float / (step_float + 16.0)
    new_in_momentum = 0.5 * in_momentum + grad_share[:, :proj_width]
    new_out_momentum = 0.5 * out_momentum + jnp.transpose(grad_share[:, proj_width:])
    first_row = lax.axis_index("seq") * share_rows
    own_in = lax.dynamic_slice_in_dim(in_weight, first_row, share_rows, 0).astype(jnp.float32)
    own_out = lax.dynamic_slice_in_dim(out_weight, first_row, share_rows, 1).astype(jnp.float32)
    new_in_part = (own_in - rate_now * new_in_momentum).astype(jnp.bfloat16)
    new_out_part = (own_out - rate_now * new_out_momentum).astype(jnp.bfloat16)
    new_in_weight, new_out_weight = (
        lax.all_gather(new_in_part, "seq", axis=0, tiled=True),
        lax.all_gather(new_out_part, "seq", axis=1, tiled=True),
    )
    (
        norm_gain_total,
        conv_weight_total,
        conv_bias_total,
        dt_bias_total,
        a_log_total,
        skip_total,
        gate_gain_total,
        out_square_total,
        mix_square_total,
        valid_total,
    ) = lax.psum(
        (
            norm_gain_grad,
            conv_weight_grad,
            conv_bias_grad,
            dt_bias_grad,
            a_log_grad,
            skip_grad,
            gate_gain_grad,
            out_square,
            mix_square,
            valid_count,
        ),
        ("dp", "seq"),
    )
    denominator = jnp.maximum(valid_total, 1.0) * model_width
    output_rms = jnp.sqrt(out_square_total / denominator).reshape(1)
    mixer_rms = jnp.sqrt(mix_square_total / denominator).reshape(1)
    return (
        block_out.astype(jnp.bfloat16),
        input_grad,
        new_in_weight,
        new_out_weight,
        new_in_momentum,
        new_out_momentum,
        norm_gain_total,
        conv_weight_total,
        conv_bias_total,
        dt_bias_total,
        a_log_total,
        skip_total,
        gate_gain_total,
        output_rms,
        mixer_rms,
    )


def solution(mesh):
    placed = (
        P("dp", "seq", None),
        P("dp", "seq", None),
        P("dp", "seq"),
        P("dp", "seq"),
        P("dp", "seq"),
        P(),
        P(),
        P(),
        P(),
        P(),
        P(),
        P(),
        P(),
        P(),
        P(),
        P(),
        P("seq", None),
        P(None, "seq"),
    )
    return jax.shard_map(
        local,
        mesh=mesh,
        in_specs=placed,
        out_specs=(
            P("dp", "seq", None),
            P("dp", "seq", None),
            P(),
            P(),
            P("seq", None),
            P(None, "seq"),
            P(),
            P(),
            P(),
            P(),
            P(),
            P(),
            P(),
            P(),
            P(),
        ),
        check_vma=False,
    )
```

profile of v0, /device:TPU:0, one launch (start us, length us, event | category | flops | bytes accessed | tf_op | source)
XLA Modules:
  0.0 885.2 jit_solution(818629642145929513)
XLA Ops:
  9.2 5.5 convolution_bitcast_fusion
  14.8 4.9 collective-permute-start
  19.9 3.5 collective-permute-start.1
  25.9 4.2 slice.132
  36.3 11.6 %fusion.26 = (f32[1,512,1792]{2,1,0:T(8,128)S(1)}, f32[1,512,1792]{2,1,0:T(8,128)}) fusion(f32[1792]{0:T(1024)S(1)} %get-tuple-element.401, f32[1,512,1792]{2,1,0:T(8,128)} %slice.132, f32[512]{0:T(512)S(1)} %bitcast.377, f32[1792]{0:T(1024)S(1)} %get-tuple-element.402, f32[512]{0:T(512)S(1)} %bitcast.374, f32[1,3,1792]{2,1,0:T(4,128)S(1)} %copy.241, ...), kind=kLoop, calls=%fused_computation.50 | loop fusion | flops 17432576 | bytes 11075584 | tf_op jit(solution)/shard_map/jvp(jit(silu))/mul | solution.py:120
  49.8 2.1 slice.142
  51.9 2.4 copy.242
  54.3 4.3 fusion.70
  65.2 2.9 mul.637
  68.0 3.5 copy.254
  71.5 9.9 %all_gather.26 = bf16[4,1,24]{2,1,0:T(2,128)(2,1)} all-gather(bf16[1,1,24]{2,1,0:T(2,128)(2,1)} %get-tuple-element.453), channel_id=1, replica_groups=mesh['dp'=8,'seq'=4] {'seq'}, dimensions={0}, use_global_device_ids=true | all-gather | bytes 240 | tf_op jit(solution)/shard_map/all_gather | solution.py:19
  84.5 3.0 fusion.111
  87.5 7.6 all-gather.11.cloned.1.call-done
  96.4 4.0 fusion.88
  100.5 29.3 %fusion.30 = f32[1,512,24,64]{1,3,2,0:T(8,128)} fusion(f32[1,512,24,64]{1,3,2,0:T(8,128)S(1)} %bitcast.337, f32[512,24,64]{0,2,1:T(8,128)S(1)} %fusion.88, f32[24]{0:T(128)S(1)} %copy-done.89, f32[512,24]{0,1:T(8,128)S(1)} %copy-done.35, f32[24,512]{1,0:T(8,128)S(1)} %copy-done.45, f32[512,512]{1,0:T(8,128)S(1)} %copy-done.27, ...), kind=kOutput, calls=%fused_computation.59 | convolution fusion | flops 4854644736 | bytes 14041184 | tf_op jit(solution)/shard_map/jvp(shtu,suhp->sthp)/dot_general | solution.py:157
  129.8 3.6 copy.252
  133.4 4.0 multiply_reduce_fusion.7
  137.4 2.3 fusion.31
  141.5 5.6 multiply_reduce_fusion.5
  148.8 2.2 mul.669
  151.0 12.4 %copy.255 = f32[1,512,1536]{1,2,0:T(8,128)} copy(f32[1,512,1536]{2,1,0:T(8,128)} %mul.669) | data formatting | bytes 6291456 | tf_op jit(solution)/shard_map/transpose(jvp())/mul | solution.py:162
  163.4 5.4 fusion.107
  168.9 17.8 %all_gather.29 = f32[4,1,24]{2,1,0:T(1,128)} all-gather(f32[1,1,24]{2,1,0:T(1,128)S(1)} %copy-done.87), channel_id=1, replica_groups=mesh['dp'=8,'seq'=4] {'seq'}, dimensions={0}, use_global_device_ids=true | all-gather | bytes 480 | tf_op jit(solution)/shard_map/all_gather | solution.py:38
  186.7 3.5 copy.256
  190.2 3.7 multiply_reduce_fusion.6
  194.8 33.7 %fusion.7 = (f32[24,512]{1,0:T(8,128)}, f32[24,512]{1,0:T(8,128)S(1)}, f32[512,512]{1,0:T(8,128)}) fusion(f32[24,512]{1,0:T(8,128)} %bitcast_add_fusion.6, f32[512,512]{1,0:T(8,128)} %fusion.111, pred[512,512]{1,0:T(8,128)(4,1)} %fusion.81, f32[24,64,512]{2,1,0:T(8,128)} %bitcast.346, f32[512,24,64]{0,2,1:T(8,128)S(1)} %bitcast.339, f32[512,24]{0,1:T(8,128)} %copy.243), kind=kOutput, calls=%fused_computation.12 | convolution fusion | flops 4888961024 | bytes 8847360 | tf_op jit(solution)/shard_map/transpose(jvp(shtu,suhp->sthp))/dot_general | solution.py:157
  230.9 3.9 convolution_bitcast_fusion.1
  234.9 7.1 convolution_bitcast_fusion.2
  242.0 2.6 fusion.79
  244.7 3.9 fusion.91
  248.6 22.4 %fusion.2 = f32[24,64,512]{2,1,0:T(8,128)} fusion(f32[24,64,512]{2,1,0:T(8,128)S(1)} %bitcast.347, f32[24,512]{1,0:T(8,128)S(1)} %copy-done.46, f32[512,512]{1,0:T(8,128)S(1)} %copy-done.28, pred[512,512]{1,0:T(8,128)(4,1)S(1)} %copy-done.33), kind=kOutput, calls=%fused_computation.9 | convolution fusion | flops 4850712576 | bytes 7651328 | tf_op jit(solution)/shard_map/transpose(jvp(shtu,suhp->sthp))/dot_general | solution.py:157
  271.0 12.0 %while.29 = (s32[]{:T(128)}, f32[1,24,64,128]{3,2,1,0:T(8,128)}, s32[]{:T(128)}, f32[4,1,24]{2,1,0:T(1,128)}, f32[4,1,24,64,128]{4,3,2,1,0:T(8,128)}, /*index=5*/s32[]{:T(128)}, s32[]{:T(128)}, s32[]{:T(128)}, s32[]{:T(128)}) while((s32[]{:T(128)}, f32[1,24,64,128]{3,2,1,0:T(8,128)}, s32[]{:T(128)}, f32[4,1,24]{2,1,0:T(1,128)}, ...), condition=%wide.region_11.12_spmd.clone, body=%wide.region_10.11_spmd.clone.sunk | while | flops 786440 | bytes 2359751 | solution.py:51
  271.5 2.2 fusion.159
  274.3 2.4 fusion.159
  277.4 2.4 fusion.159
  280.4 2.4 fusion.159
  283.0 4.1 fusion.34
  288.0 5.8 fusion.76
  293.8 4.2 fusion.33
  298.0 2.4 copy.260
  300.5 11.2 %multiply_reduce_fusion.3 = (f32[1792]{0:T(1024)}, f32[1792]{0:T(1024)S(1)}, f32[1792]{0:T(1024)}, f32[1792]{0:T(1024)S(1)}, f32[1792]{0:T(1024)}, /*index=5*/f32[1,512,1792]{2,1,0:T(8,128)S(1)}) fusion(f32[1,512,1792]{2,1,0:T(8,128)} %slice.132, f32[1,3,1792]{2,1,0:T(4,128)S(1)} %copy.241, f32[512]{0:T(512)S(1)} %bitcast.375, f32[512]{0:T(512)S(1)} %bitcast.369, ...), kind=kLoop, calls=%fused_computation.43 | loop fusion | flops 24763648 | bytes 18415616 | tf_op jit(solution)/shard_map/transpose(jvp())/reduce_sum | solution.py:119
  314.5 1.9 copy-done.12
  319.6 5.0 reduce-window.36
  324.8 5.0 reduce-window.34
  331.9 2.5 fusion.48
  334.5 3.1 fusion.68
  337.7 5.8 pad_maximum_fusion
  343.4 15.2 %copy.289 = f32[768,4888]{1,0:T(8,128)} copy(f32[768,4888]{0,1:T(8,128)} %pad_maximum_fusion) | data formatting | bytes 30031872
  358.6 256.6 %reduce-scatter.4.cloned.1.call-done = f32[192,4888]{1,0:T(8,128)} async-done(((f32[768,4888]{1,0:T(8,128)}), f32[192,4888]{1,0:T(8,128)}) %reduce-scatter.4.cloned.1.call-update) | async-done | bytes 3754000
  615.2 5.7 copy.290
  622.9 89.6 %all-reduce.16.cloned.1.call-done = f32[192,4888]{0,1:T(8,128)} async-done(((f32[192,4888]{0,1:T(8,128)}), f32[192,4888]{0,1:T(8,128)}) %all-reduce.16.cloned.1.call-update) | async-done | bytes 3754000 | tf_op jit(solution)/shard_map/psum | solution.py:241
  712.5 3.5 subtract_convert_fusion.1
  717.1 3.6 copy.270
  720.7 6.4 subtract_convert_fusion
  727.1 3.8 copy.272
  731.3 3.3 multiply_reduce_fusion.8
  734.9 7.1 fusion.50
  742.6 42.8 %all-reduce.13 = (f32[768]{0:T(1024)}, f32[4,1792]{1,0:T(4,128)}, f32[1792]{0:T(1024)}, f32[24]{0:T(128)}, f32[24]{0:T(128)}, /*index=5*/f32[24]{0:T(128)}, f32[1536]{0:T(1024)}, f32[]{:T(128)}, f32[]{:T(128)}, f32[]{:T(128)}) all-reduce(f32[768]{0:T(1024)S(1)} %get-tuple-element.396, ...), channel_id=1, replica_groups=mesh['dp'=8,'seq'=4] {'dp','seq'}, use_global_device_ids=true, to_apply=%region_26.27 | all-reduce | flops 11339 | bytes 90712 | tf_op jit(solution)/shard_map/psum | solution.py:267
  787.5 3.3 fusion.52
  790.8 2.9 copy.277
  793.7 2.9 copy.278
  796.5 4.3 copy.276
  800.8 66.9 %all-gather.7.cloned.1.call-done = bf16[768,3352]{1,0:T(8,128)(2,1)} async-done(((bf16[192,3352]{1,0:T(8,128)(2,1)}), bf16[768,3352]{1,0:T(8,128)(2,1)}) %all-gather.7.cloned.1.call-update) | async-done | bytes 5148688 | tf_op jit(solution)/shard_map/all_gather | solution.py:253
  867.7 8.0 copy.275
  (290 shorter events, 42.9 us)
Async XLA Ops:
  7.2 88.0 %all-gather.11.cloned.1.call-start = ((), (), s32[]{:S(2)}) async-start(), calls=%async_computation.3 | async-start | bytes 1966080 | tf_op jit(solution)/shard_map/all_gather | solution.py:19
  9.2 5.6 copy-start.69
  9.2 10.6 %copy-start.72 = (s32[1,512]{1,0:T(1,128)S(1)}, s32[1,512]{1,0:T(1,128)}, u32[]{:S(2)}) copy-start(s32[1,512]{1,0:T(1,128)} %param.24) | copy-start | bytes 6148
  9.2 14.2 %copy-start.91 = (f32[24]{0:T(128)S(1)}, f32[24]{0:T(128)}, u32[]{:S(2)}) copy-start(f32[24]{0:T(128)} %param.34) | copy-start | bytes 292
  9.2 14.2 %copy-start.75 = (f32[24]{0:T(128)S(1)}, f32[24]{0:T(128)}, u32[]{:S(2)}) copy-start(f32[24]{0:T(128)} %param.33) | copy-start | bytes 292
  14.8 8.6 copy-start.4
  14.8 21.5 %collective-permute-start = (f32[1,3,1792]{2,0,1:T(1,128)S(1)}, f32[1,3,1792]{2,0,1:T(1,128)S(1)}, u32[]{:S(2)}, u32[]{:S(2)}) collective-permute-start(f32[1,3,1792]{2,0,1:T(1,128)S(1)} %copy.240), channel_id=1, source_target_pairs={{0,1},{1,2},{2,3},{4,5},{5,6},{6,7},{8,9},{9,10},{10,11},{12,13},{... | collective-permute-start | bytes 64520 | tf_op jit(solution)/shard_map/ppermute | solution.py:13
  19.9 16.3 %collective-permute-start.1 = (f32[1,3]{1,0:T(1,128)S(1)}, f32[1,3]{1,0:T(1,128)S(1)}, u32[]{:S(2)}, u32[]{:S(2)}) collective-permute-start(f32[1,3]{1,0:T(1,128)S(1)} %slice.135), channel_id=1, source_target_pairs={{0,1},{1,2},{2,3},{4,5},{5,6},{6,7},{8,9},{9,10},{10,11},{12,13},{... | collective-permute-start | bytes 44 | tf_op jit(solution)/shard_map/ppermute | solution.py:13
  25.8 4.3 copy-start.88
  25.8 10.2 %copy-start.63 = (f32[4,1792]{1,0:T(4,128)S(1)}, f32[4,1792]{1,0:T(4,128)}, u32[]{:S(2)}) copy-start(f32[4,1792]{1,0:T(4,128)} %param.31) | copy-start | bytes 86020
  25.8 10.5 %copy-start.74 = (f32[1792]{0:T(1024)S(1)}, f32[1792]{0:T(1024)}, u32[]{:S(2)}) copy-start(f32[1792]{0:T(1024)} %param.32) | copy-start | bytes 21508
  30.0 17.9 %copy-start.57 = (f32[1,512]{1,0:T(1,128)}, f32[1,512]{1,0:T(1,128)S(1)}, u32[]{:S(2)}) copy-start(f32[1,512]{1,0:T(1,128)S(1)} %compare_convert_fusion) | copy-start | bytes 6148
  30.8 17.1 %copy-start.62 = (s32[512]{0:T(512)}, s32[512]{0:T(512)S(1)}, u32[]{:S(2)}) copy-start(s32[512]{0:T(512)S(1)} %get-tuple-element.452) | copy-start | bytes 6148
  36.1 11.8 %copy-start.41 = (f32[1792]{0:T(1024)}, f32[1792]{0:T(1024)S(1)}, u32[]{:S(2)}) copy-start(f32[1792]{0:T(1024)S(1)} %get-tuple-element.401) | copy-start | bytes 21508
  36.2 11.8 %copy-start.43 = (f32[1792]{0:T(1024)}, f32[1792]{0:T(1024)S(1)}, u32[]{:S(2)}) copy-start(f32[1792]{0:T(1024)S(1)} %get-tuple-element.402) | copy-start | bytes 21508
  36.3 11.7 %copy-start.51 = (f32[1,512]{1,0:T(1,128)}, f32[1,512]{1,0:T(1,128)S(1)}, u32[]{:S(2)}) copy-start(f32[1,512]{1,0:T(1,128)S(1)} %get-tuple-element.470) | copy-start | bytes 6148
  36.3 11.7 %copy-start.53 = (f32[1,512]{1,0:T(1,128)}, f32[1,512]{1,0:T(1,128)S(1)}, u32[]{:S(2)}) copy-start(f32[1,512]{1,0:T(1,128)S(1)} %get-tuple-element.471) | copy-start | bytes 6148
  36.3 11.7 %copy-start.55 = (f32[1,512]{1,0:T(1,128)}, f32[1,512]{1,0:T(1,128)S(1)}, u32[]{:S(2)}) copy-start(f32[1,512]{1,0:T(1,128)S(1)} %get-tuple-element.472) | copy-start | bytes 6148
  58.7 212.3 %all-gather.13.cloned.1.call-start = ((), (), s32[]{:S(2)}) async-start(), calls=%async_computation.4 | async-start | bytes 3932160 | tf_op jit(solution)/shard_map/all_gather | solution.py:38
  100.4 29.4 %copy-start.14 = (f32[512,24,64]{0,2,1:T(8,128)}, f32[512,24,64]{0,2,1:T(8,128)S(1)}, u32[]{:S(2)}) copy-start(f32[512,24,64]{0,2,1:T(8,128)S(1)} %fusion.88) | copy-start | bytes 9437188
  137.4 4.1 copy-start.5
  141.5 7.3 copy-start.15
  163.4 5.5 copy-start.87
  168.8 446.4 %reduce-scatter.4.cloned.1.call-start = ((), (), s32[]{:S(2)}) async-start(), calls=%async_computation.6 | async-start | bytes 19169280
  230.9 11.1 %copy-start.18 = (f32[512,512]{1,0:T(8,128)S(1)}, f32[512,512]{1,0:T(8,128)}, u32[]{:S(2)}) copy-start(f32[512,512]{1,0:T(8,128)} %get-tuple-element.388) | copy-start | bytes 3145732
  230.9 13.7 %copy-start.7 = (f32[1,512,1536]{2,1,0:T(8,128)S(1)}, f32[1,512,1536]{2,1,0:T(8,128)}, u32[]{:S(2)}) copy-start(f32[1,512,1536]{2,1,0:T(8,128)} %copy-done.6) | copy-start | bytes 9437188
  230.9 13.7 %copy-start.17 = (bf16[1,512,768]{2,1,0:T(8,128)(2,1)S(1)}, bf16[1,512,768]{2,1,0:T(8,128)(2,1)}, u32[]{:S(2)}) copy-start(bf16[1,512,768]{2,1,0:T(8,128)(2,1)} %param.23) | copy-start | bytes 2359300
  230.9 13.7 %copy-start.48 = (f32[1536]{0:T(1024)S(1)}, f32[1536]{0:T(1024)}, u32[]{:S(2)}) copy-start(f32[1536]{0:T(1024)} %param.36) | copy-start | bytes 18436
  230.9 13.7 %copy-start.65 = (f32[512]{0:T(512)S(1)}, f32[512]{0:T(512)}, u32[]{:S(2)}) copy-start(f32[512]{0:T(512)} %copy-done.64) | copy-start | bytes 6148
  283.0 4.2 copy-start
  283.0 4.2 copy-start.1
  283.0 5.0 copy-start.29
  283.0 10.8 %copy-start.21 = (f32[24,64,512]{2,1,0:T(8,128)S(1)}, f32[24,64,512]{2,1,0:T(8,128)}, u32[]{:S(2)}) copy-start(f32[24,64,512]{2,1,0:T(8,128)} %fusion.2) | copy-start | bytes 9437188
  287.2 6.6 copy-start.11
  287.2 6.6 copy-start.37
  287.2 6.6 copy-start.90
  300.5 11.2 %copy-start.42 = (f32[1792]{0:T(1024)S(1)}, f32[1792]{0:T(1024)}, u32[]{:S(2)}) copy-start(f32[1792]{0:T(1024)} %copy-done.41) | copy-start | bytes 21508
  300.5 11.2 %copy-start.44 = (f32[1792]{0:T(1024)S(1)}, f32[1792]{0:T(1024)}, u32[]{:S(2)}) copy-start(f32[1792]{0:T(1024)} %copy-done.43) | copy-start | bytes 21508
  313.3 4.7 copy-start.30
  313.4 4.7 copy-start.31
  313.4 4.7 copy-start.76
  313.4 4.7 copy-start.78
  313.4 4.7 copy-start.80
  313.4 4.7 copy-start.82
  313.4 6.0 copy-start.86
  316.4 13.7 %copy-start.38 = (f32[512,24]{0,1:T(8,128)S(1)}, f32[512,24]{0,1:T(8,128)}, u32[]{:S(2)}) copy-start(f32[512,24]{0,1:T(8,128)} %get-tuple-element.466) | copy-start | bytes 147460
  316.4 13.9 %copy-start.85 = (f32[24]{0:T(128)S(1)}, f32[24]{0:T(128)}, u32[]{:S(2)}) copy-start(f32[24]{0:T(128)} %copy-done.84) | copy-start | bytes 292
  316.5 15.4 %collective-permute-start.2 = (bf16[1,3,1792]{2,1,0:T(4,128)(2,1)S(1)}, bf16[1,3,1792]{2,1,0:T(4,128)(2,1)S(1)}, u32[]{:S(2)}, u32[]{:S(2)}) collective-permute-start(bf16[1,3,1792]{2,1,0:T(4,128)(2,1)S(1)} %slice.284), channel_id=1, source_target_pairs={{1,0},{2,1},{3,2},{5,4},{6,5},{7,6},{9,8},{10,9},{11,10},{13,12},{... | collective-permute-start | bytes 32264 | tf_op jit(solution)/shard_map/ppermute | solution.py:13
  330.3 4.1 copy-start.19
  330.3 4.1 copy-start.24
  330.4 4.1 copy-start.70
  330.4 4.1 copy-start.83
  331.9 5.7 copy-start.39
  331.9 5.7 slice-start
  358.6 353.9 %all-reduce.16.cloned.1.call-start = ((), (), s32[]{:S(2)}) async-start(), calls=%async_computation.5 | async-start | bytes 10010624 | tf_op jit(solution)/shard_map/psum | solution.py:241
  621.0 175.6 %all-gather.9.cloned.1.call-start = ((), (), s32[]{:S(2)}) async-start(), calls=%async_computation.2 | async-start | bytes 2949120 | tf_op jit(solution)/shard_map/all_gather | solution.py:254
  717.1 150.7 %all-gather.7.cloned.1.call-start = ((), (), s32[]{:S(2)}) async-start(), calls=%async_computation.1 | async-start | bytes 6635520 | tf_op jit(solution)/shard_map/all_gather | solution.py:253
  727.1 4.1 copy-start.8
  727.1 4.1 copy-start.49
  727.1 4.1 copy-start.66
  734.8 7.2 copy-start.73
  734.8 7.8 copy-start.71
  734.9 52.6 %copy-start.68 = (f32[512]{0:T(512)S(1)}, f32[512]{0:T(512)}, u32[]{:S(2)}) copy-start(f32[512]{0:T(512)} %copy-done.67) | copy-start | bytes 6148
  742.0 48.8 %copy-start.13 = (f32[192,3352]{0,1:T(8,128)S(1)}, f32[192,3352]{0,1:T(8,128)}, u32[]{:S(2)}) copy-start(f32[192,3352]{0,1:T(8,128)} %get-tuple-element.444) | copy-start | bytes 7723012
  (40 other events, 122.4 us)
Sparse Core Ops, SparseCore 0:
  58.8 36.3 all-gather.10
  169.0 70.9 all-gather.12
  358.7 256.4 reduce-scatter.3
  621.1 91.3 all-reduce.15
  717.2 50.9 all-gather.8
  769.7 98.0 all-gather.6
where the time goes:
time: 895 us; the launch traced here: 885 us
  waiting for transfers between devices  421 us (47%)
  matrix products  151 us (17%)
  local copies, waits for them, and re-layouts  108 us (12%)
  other arithmetic  101 us (11%)
  blocking collectives  70.5 us (8%)
  between operations  23.1 us (3%)
  starting transfers between devices  10.1 us (1%)
    unnamed x7, waiting for transfers between devices  257 us
    psum x1, waiting for transfers between devices, local(): whole_grad = lax.psum(jnp.concatenate([in_part, out_part], axis=1), 'dp')  89.6 us
    dot_general x3, matrix products, piece_out(): jnp.einsum('shtu,suhp->sthp', weighted, signal_in * step_in[..., None], p...  85.3 us
    all_gather x1, waiting for transfers between devices, local(): lax.all_gather(new_in_part, 'seq', axis=0, tiled=True)  66.9 us
    unnamed x198, local copies, waits for them, and re-layouts  51 us
    psum x1, blocking collectives, local(): lax.psum((norm_gain_grad, conv_weight_grad, conv_bias_grad, dt_bias_grad,...  42.8 us
    mul x4, local copies, waits for them, and re-layouts, piece_out(): jnp.einsum('stn,shpn->sthp', reader_in, incoming_in, precision=highest)  20.4 us
  transfers between devices with their start and end apart: 9, of which 4 were waited for; matrix products, arithmetic and copies ran while one was open for 19% of the time, Pallas kernels for 0%

commit v1 on v0

--- a/solution.py
+++ b/solution.py
@@ -265,19 +265,22 @@
         mix_square_total,
         valid_total,
     ) = lax.psum(
-        (
-            norm_gain_grad,
-            conv_weight_grad,
-            conv_bias_grad,
-            dt_bias_grad,
-            a_log_grad,
-            skip_grad,
-            gate_gain_grad,
-            out_square,
-            mix_square,
-            valid_count,
+        lax.psum(
+            (
+                norm_gain_grad,
+                conv_weight_grad,
+                conv_bias_grad,
+                dt_bias_grad,
+                a_log_grad,
+                skip_grad,
+                gate_gain_grad,
+                out_square,
+                mix_square,
+                valid_count,
+            ),
+            "seq",
         ),
-        ("dp", "seq"),
+        "dp",
     )
     denominator = jnp.maximum(valid_total, 1.0) * model_width
     output_rms = jnp.sqrt(out_square_total / denominator).reshape(1)

time: 895 us -> 897 us (level)
    psum x0 -> x1, blocking collectives: none -> 23.5 us  [local(): lax.psum(lax.psum((norm_gain_grad, conv_weight_grad, conv_bias_grad, dt_b...]
    psum x1, blocking collectives: 42.8 us -> 22.5 us  [local(): lax.psum((norm_gain_grad, conv_weight_grad, conv_bias_grad, dt_bias_grad,...]
    unnamed x198 -> x202, local copies, waits for them, and re-layouts: 51 us -> 51 us
where the time goes in v1:
time: 897 us; the launch traced here: 887 us
  waiting for transfers between devices  417 us (46%)
  matrix products  152 us (17%)
  local copies, waits for them, and re-layouts  108 us (12%)
  other arithmetic  103 us (11%)
  blocking collectives  73.7 us (8%)
  between operations  23.1 us (3%)
  starting transfers between devices  10.1 us (1%)
    unnamed x7, waiting for transfers between devices  257 us
    psum x1, waiting for transfers between devices, local(): whole_grad = lax.psum(jnp.concatenate([in_part, out_part], axis=1), 'dp')  89.6 us
    dot_general x3, matrix products, piece_out(): jnp.einsum('shtu,suhp->sthp', weighted, signal_in * step_in[..., None], p...  85.3 us
    all_gather x1, waiting for transfers between devices, local(): lax.all_gather(new_in_part, 'seq', axis=0, tiled=True)  62.7 us
    unnamed x202, local copies, waits for them, and re-layouts  51 us
    psum x1, blocking collectives, local(): lax.psum(lax.psum((norm_gain_grad, conv_weight_grad, conv_bias_grad, dt_b...  23.5 us
    psum x1, blocking collectives, local(): lax.psum((norm_gain_grad, conv_weight_grad, conv_bias_grad, dt_bias_grad,...  22.5 us
    mul x4, local copies, waits for them, and re-layouts, piece_out(): jnp.einsum('stn,shpn->sthp', reader_in, incoming_in, precision=highest)  20.4 us
  transfers between devices with their start and end apart: 9, of which 4 were waited for; matrix products, arithmetic and copies ran while one was open for 19% of the time, Pallas kernels for 0%

profile of v1, /device:TPU:0, one launch (start us, length us, event | category | flops | bytes accessed | tf_op | source)
XLA Modules:
  0.0 887.1 jit_solution(10664106403683028865)
XLA Ops:
  9.2 5.5 convolution_bitcast_fusion
  14.8 4.9 collective-permute-start
  19.9 3.5 collective-permute-start.1
  25.9 4.2 slice.132
  36.3 11.6 %fusion.26 = (f32[1,512,1792]{2,1,0:T(8,128)S(1)}, f32[1,512,1792]{2,1,0:T(8,128)}) fusion(f32[1792]{0:T(1024)S(1)} %get-tuple-element.401, f32[1,512,1792]{2,1,0:T(8,128)} %slice.132, f32[512]{0:T(512)S(1)} %bitcast.377, f32[1792]{0:T(1024)S(1)} %get-tuple-element.402, f32[512]{0:T(512)S(1)} %bitcast.374, f32[1,3,1792]{2,1,0:T(4,128)S(1)} %copy.241, ...), kind=kLoop, calls=%fused_computation.50 | loop fusion | flops 17432576 | bytes 11075584 | tf_op jit(solution)/shard_map/jvp(jit(silu))/mul | solution.py:120
  49.8 2.1 slice.142
  51.9 2.4 copy.242
  54.3 4.3 fusion.70
  65.2 2.9 mul.637
  68.0 3.5 copy.254
  71.5 9.9 %all_gather.26 = bf16[4,1,24]{2,1,0:T(2,128)(2,1)} all-gather(bf16[1,1,24]{2,1,0:T(2,128)(2,1)} %get-tuple-element.463), channel_id=1, replica_groups=mesh['dp'=8,'seq'=4] {'seq'}, dimensions={0}, use_global_device_ids=true | all-gather | bytes 240 | tf_op jit(solution)/shard_map/all_gather | solution.py:19
  84.5 3.0 fusion.111
  87.5 7.6 all-gather.11.cloned.1.call-done
  96.4 4.0 fusion.88
  100.5 29.3 %fusion.30 = f32[1,512,24,64]{1,3,2,0:T(8,128)} fusion(f32[1,512,24,64]{1,3,2,0:T(8,128)S(1)} %bitcast.337, f32[512,24,64]{0,2,1:T(8,128)S(1)} %fusion.88, f32[24]{0:T(128)S(1)} %copy-done.91, f32[512,24]{0,1:T(8,128)S(1)} %copy-done.35, f32[24,512]{1,0:T(8,128)S(1)} %copy-done.45, f32[512,512]{1,0:T(8,128)S(1)} %copy-done.27, ...), kind=kOutput, calls=%fused_computation.59 | convolution fusion | flops 4854644736 | bytes 14041184 | tf_op jit(solution)/shard_map/jvp(shtu,suhp->sthp)/dot_general | solution.py:157
  129.8 3.6 copy.252
  133.4 4.0 multiply_reduce_fusion.7
  137.4 2.3 fusion.31
  141.5 5.6 multiply_reduce_fusion.5
  148.8 2.2 mul.669
  151.0 12.4 %copy.255 = f32[1,512,1536]{1,2,0:T(8,128)} copy(f32[1,512,1536]{2,1,0:T(8,128)} %mul.669) | data formatting | bytes 6291456 | tf_op jit(solution)/shard_map/transpose(jvp())/mul | solution.py:162
  163.4 5.4 fusion.107
  168.9 17.8 %all_gather.29 = f32[4,1,24]{2,1,0:T(1,128)} all-gather(f32[1,1,24]{2,1,0:T(1,128)S(1)} %copy-done.89), channel_id=1, replica_groups=mesh['dp'=8,'seq'=4] {'seq'}, dimensions={0}, use_global_device_ids=true | all-gather | bytes 480 | tf_op jit(solution)/shard_map/all_gather | solution.py:38
  186.7 3.5 copy.256
  190.2 3.7 multiply_reduce_fusion.6
  194.8 33.7 %fusion.7 = (f32[24,512]{1,0:T(8,128)}, f32[24,512]{1,0:T(8,128)S(1)}, f32[512,512]{1,0:T(8,128)}) fusion(f32[24,512]{1,0:T(8,128)} %bitcast_add_fusion.6, f32[512,512]{1,0:T(8,128)} %fusion.111, pred[512,512]{1,0:T(8,128)(4,1)} %fusion.81, f32[24,64,512]{2,1,0:T(8,128)} %bitcast.346, f32[512,24,64]{0,2,1:T(8,128)S(1)} %bitcast.339, f32[512,24]{0,1:T(8,128)} %copy.243), kind=kOutput, calls=%fused_computation.12 | convolution fusion | flops 4888961024 | bytes 8847360 | tf_op jit(solution)/shard_map/transpose(jvp(shtu,suhp->sthp))/dot_general | solution.py:157
  230.9 3.9 convolution_bitcast_fusion.1
  234.9 7.1 convolution_bitcast_fusion.2
  242.0 2.6 fusion.79
  244.7 3.9 fusion.91
  248.6 22.4 %fusion.2 = f32[24,64,512]{2,1,0:T(8,128)} fusion(f32[24,64,512]{2,1,0:T(8,128)S(1)} %bitcast.347, f32[24,512]{1,0:T(8,128)S(1)} %copy-done.46, f32[512,512]{1,0:T(8,128)S(1)} %copy-done.28, pred[512,512]{1,0:T(8,128)(4,1)S(1)} %copy-done.33), kind=kOutput, calls=%fused_computation.9 | convolution fusion | flops 4850712576 | bytes 7651328 | tf_op jit(solution)/shard_map/transpose(jvp(shtu,suhp->sthp))/dot_general | solution.py:157
  271.0 12.0 %while.29 = (s32[]{:T(128)}, f32[1,24,64,128]{3,2,1,0:T(8,128)}, s32[]{:T(128)}, f32[4,1,24]{2,1,0:T(1,128)}, f32[4,1,24,64,128]{4,3,2,1,0:T(8,128)}, /*index=5*/s32[]{:T(128)}, s32[]{:T(128)}, s32[]{:T(128)}, s32[]{:T(128)}) while((s32[]{:T(128)}, f32[1,24,64,128]{3,2,1,0:T(8,128)}, s32[]{:T(128)}, f32[4,1,24]{2,1,0:T(1,128)}, ...), condition=%wide.region_11.12_spmd.clone, body=%wide.region_10.11_spmd.clone.sunk | while | flops 786440 | bytes 2359751 | solution.py:51
  271.5 2.2 fusion.159
  274.3 2.4 fusion.159
  277.4 2.4 fusion.159
  280.4 2.4 fusion.159
  283.0 4.1 fusion.34
  288.0 5.8 fusion.76
  293.8 4.2 fusion.33
  298.0 2.4 copy.260
  300.5 11.2 %multiply_reduce_fusion.3 = (f32[1792]{0:T(1024)}, f32[1792]{0:T(1024)S(1)}, f32[1792]{0:T(1024)}, f32[1792]{0:T(1024)S(1)}, f32[1792]{0:T(1024)}, /*index=5*/f32[1,512,1792]{2,1,0:T(8,128)S(1)}) fusion(f32[1,512,1792]{2,1,0:T(8,128)} %slice.132, f32[1,3,1792]{2,1,0:T(4,128)S(1)} %copy.241, f32[512]{0:T(512)S(1)} %bitcast.375, f32[512]{0:T(512)S(1)} %bitcast.369, ...), kind=kLoop, calls=%fused_computation.43 | loop fusion | flops 24763648 | bytes 18415616 | tf_op jit(solution)/shard_map/transpose(jvp())/reduce_sum | solution.py:119
  319.6 5.0 reduce-window.36
  324.8 5.0 reduce-window.34
  332.4 2.5 fusion.48
  335.0 3.1 fusion.68
  338.1 5.8 pad_maximum_fusion
  343.9 15.2 %copy.289 = f32[768,4888]{1,0:T(8,128)} copy(f32[768,4888]{0,1:T(8,128)} %pad_maximum_fusion) | data formatting | bytes 30031872
  359.1 256.6 %reduce-scatter.4.cloned.1.call-done = f32[192,4888]{1,0:T(8,128)} async-done(((f32[768,4888]{1,0:T(8,128)}), f32[192,4888]{1,0:T(8,128)}) %reduce-scatter.4.cloned.1.call-update) | async-done | bytes 3754000
  615.7 5.7 copy.290
  623.4 89.6 %all-reduce.17.cloned.1.call-done = f32[192,4888]{0,1:T(8,128)} async-done(((f32[192,4888]{0,1:T(8,128)}), f32[192,4888]{0,1:T(8,128)}) %all-reduce.17.cloned.1.call-update) | async-done | bytes 3754000 | tf_op jit(solution)/shard_map/psum | solution.py:241
  713.0 3.5 subtract_convert_fusion.1
  717.6 3.6 copy.270
  721.2 6.4 subtract_convert_fusion
  727.6 3.8 copy.272
  732.3 3.3 multiply_reduce_fusion.8
  736.4 7.8 fusion.50
  744.7 22.5 %all-reduce.14 = (f32[768]{0:T(1024)S(1)}, f32[4,1792]{1,0:T(4,128)S(1)}, f32[1792]{0:T(1024)S(1)}, f32[24]{0:T(128)}, f32[24]{0:T(128)}, /*index=5*/f32[24]{0:T...) all-reduce(f32[768]{0:T(1024)S(1)} %get-tuple-element.396, ...), channel_id=1, replica_groups=mesh['dp'=8,'seq'=4] {'seq'}, use_global_device_ids=true, to_apply=%region_26.27 | all-reduce | flops 11339 | bytes 90712 | tf_op jit(solution)/shard_map/psum | solution.py:268
  767.3 23.5 %all-reduce.13 = (f32[768]{0:T(1024)}, f32[4,1792]{1,0:T(4,128)}, f32[1792]{0:T(1024)}, f32[24]{0:T(128)}, f32[24]{0:T(128)}, /*index=5*/f32[24]{0:T(128)}, f32[1536]{0:T(1024)}, f32[]{:T(128)}, f32[]{:T(128)}, f32[]{:T(128)}) all-reduce(f32[768]{0:T(1024)S(1)} %get-tuple-element.436, ...), channel_id=1, replica_groups=mesh['dp'=8,'seq'=4] {'dp'}, use_global_device_ids=true, to_apply=%region_27.28 | all-reduce | flops 11339 | bytes 90712 | tf_op jit(solution)/shard_map/psum | solution.py:267
  793.5 3.3 fusion.52
  796.9 2.9 copy.277
  799.7 2.9 copy.278
  802.6 4.3 copy.276
  806.9 62.7 %all-gather.7.cloned.1.call-done = bf16[768,3352]{1,0:T(8,128)(2,1)} async-done(((bf16[192,3352]{1,0:T(8,128)(2,1)}), bf16[768,3352]{1,0:T(8,128)(2,1)}) %all-gather.7.cloned.1.call-update) | async-done | bytes 5148688 | tf_op jit(solution)/shard_map/all_gather | solution.py:253
  869.6 8.0 copy.275
  (295 shorter events, 47.0 us)
Async XLA Ops:
  7.2 88.0 %all-gather.11.cloned.1.call-start = ((), (), s32[]{:S(2)}) async-start(), calls=%async_computation.3 | async-start | bytes 1966080 | tf_op jit(solution)/shard_map/all_gather | solution.py:19
  9.2 5.6 copy-start.69
  9.2 10.6 %copy-start.72 = (s32[1,512]{1,0:T(1,128)S(1)}, s32[1,512]{1,0:T(1,128)}, u32[]{:S(2)}) copy-start(s32[1,512]{1,0:T(1,128)} %param.24) | copy-start | bytes 6148
  9.2 14.2 %copy-start.93 = (f32[24]{0:T(128)S(1)}, f32[24]{0:T(128)}, u32[]{:S(2)}) copy-start(f32[24]{0:T(128)} %param.34) | copy-start | bytes 292
  9.2 14.2 %copy-start.75 = (f32[24]{0:T(128)S(1)}, f32[24]{0:T(128)}, u32[]{:S(2)}) copy-start(f32[24]{0:T(128)} %param.33) | copy-start | bytes 292
  14.8 8.6 copy-start.4
  14.8 21.5 %collective-permute-start = (f32[1,3,1792]{2,0,1:T(1,128)S(1)}, f32[1,3,1792]{2,0,1:T(1,128)S(1)}, u32[]{:S(2)}, u32[]{:S(2)}) collective-permute-start(f32[1,3,1792]{2,0,1:T(1,128)S(1)} %copy.240), channel_id=1, source_target_pairs={{0,1},{1,2},{2,3},{4,5},{5,6},{6,7},{8,9},{9,10},{10,11},{12,13},{... | collective-permute-start | bytes 64520 | tf_op jit(solution)/shard_map/ppermute | solution.py:13
  19.9 16.3 %collective-permute-start.1 = (f32[1,3]{1,0:T(1,128)S(1)}, f32[1,3]{1,0:T(1,128)S(1)}, u32[]{:S(2)}, u32[]{:S(2)}) collective-permute-start(f32[1,3]{1,0:T(1,128)S(1)} %slice.135), channel_id=1, source_target_pairs={{0,1},{1,2},{2,3},{4,5},{5,6},{6,7},{8,9},{9,10},{10,11},{12,13},{... | collective-permute-start | bytes 44 | tf_op jit(solution)/shard_map/ppermute | solution.py:13
  25.8 4.3 copy-start.90
  25.8 10.2 %copy-start.63 = (f32[4,1792]{1,0:T(4,128)S(1)}, f32[4,1792]{1,0:T(4,128)}, u32[]{:S(2)}) copy-start(f32[4,1792]{1,0:T(4,128)} %param.31) | copy-start | bytes 86020
  25.8 10.5 %copy-start.74 = (f32[1792]{0:T(1024)S(1)}, f32[1792]{0:T(1024)}, u32[]{:S(2)}) copy-start(f32[1792]{0:T(1024)} %param.32) | copy-start | bytes 21508
  30.0 17.9 %copy-start.57 = (f32[1,512]{1,0:T(1,128)}, f32[1,512]{1,0:T(1,128)S(1)}, u32[]{:S(2)}) copy-start(f32[1,512]{1,0:T(1,128)S(1)} %compare_convert_fusion) | copy-start | bytes 6148
  30.8 17.1 %copy-start.62 = (s32[512]{0:T(512)}, s32[512]{0:T(512)S(1)}, u32[]{:S(2)}) copy-start(s32[512]{0:T(512)S(1)} %get-tuple-element.462) | copy-start | bytes 6148
  36.1 11.8 %copy-start.41 = (f32[1792]{0:T(1024)}, f32[1792]{0:T(1024)S(1)}, u32[]{:S(2)}) copy-start(f32[1792]{0:T(1024)S(1)} %get-tuple-element.401) | copy-start | bytes 21508
  36.2 11.8 %copy-start.43 = (f32[1792]{0:T(1024)}, f32[1792]{0:T(1024)S(1)}, u32[]{:S(2)}) copy-start(f32[1792]{0:T(1024)S(1)} %get-tuple-element.402) | copy-start | bytes 21508
  36.3 11.7 %copy-start.51 = (f32[1,512]{1,0:T(1,128)}, f32[1,512]{1,0:T(1,128)S(1)}, u32[]{:S(2)}) copy-start(f32[1,512]{1,0:T(1,128)S(1)} %get-tuple-element.480) | copy-start | bytes 6148
  36.3 11.7 %copy-start.53 = (f32[1,512]{1,0:T(1,128)}, f32[1,512]{1,0:T(1,128)S(1)}, u32[]{:S(2)}) copy-start(f32[1,512]{1,0:T(1,128)S(1)} %get-tuple-element.481) | copy-start | bytes 6148
  36.3 11.7 %copy-start.55 = (f32[1,512]{1,0:T(1,128)}, f32[1,512]{1,0:T(1,128)S(1)}, u32[]{:S(2)}) copy-start(f32[1,512]{1,0:T(1,128)S(1)} %get-tuple-element.482) | copy-start | bytes 6148
  58.7 212.3 %all-gather.13.cloned.1.call-start = ((), (), s32[]{:S(2)}) async-start(), calls=%async_computation.4 | async-start | bytes 3932160 | tf_op jit(solution)/shard_map/all_gather | solution.py:38
  100.4 29.4 %copy-start.14 = (f32[512,24,64]{0,2,1:T(8,128)}, f32[512,24,64]{0,2,1:T(8,128)S(1)}, u32[]{:S(2)}) copy-start(f32[512,24,64]{0,2,1:T(8,128)S(1)} %fusion.88) | copy-start | bytes 9437188
  141.5 7.3 copy-start.15
  163.4 5.5 copy-start.89
  168.8 446.9 %reduce-scatter.4.cloned.1.call-start = ((), (), s32[]{:S(2)}) async-start(), calls=%async_computation.6 | async-start | bytes 19169280
  230.9 11.1 %copy-start.18 = (f32[512,512]{1,0:T(8,128)S(1)}, f32[512,512]{1,0:T(8,128)}, u32[]{:S(2)}) copy-start(f32[512,512]{1,0:T(8,128)} %get-tuple-element.388) | copy-start | bytes 3145732
  230.9 13.7 %copy-start.7 = (f32[1,512,1536]{2,1,0:T(8,128)S(1)}, f32[1,512,1536]{2,1,0:T(8,128)}, u32[]{:S(2)}) copy-start(f32[1,512,1536]{2,1,0:T(8,128)} %copy-done.6) | copy-start | bytes 9437188
  230.9 13.7 %copy-start.17 = (bf16[1,512,768]{2,1,0:T(8,128)(2,1)S(1)}, bf16[1,512,768]{2,1,0:T(8,128)(2,1)}, u32[]{:S(2)}) copy-start(bf16[1,512,768]{2,1,0:T(8,128)(2,1)} %param.23) | copy-start | bytes 2359300
  230.9 13.7 %copy-start.48 = (f32[1536]{0:T(1024)S(1)}, f32[1536]{0:T(1024)}, u32[]{:S(2)}) copy-start(f32[1536]{0:T(1024)} %param.36) | copy-start | bytes 18436
  230.9 13.7 %copy-start.65 = (f32[512]{0:T(512)S(1)}, f32[512]{0:T(512)}, u32[]{:S(2)}) copy-start(f32[512]{0:T(512)} %copy-done.64) | copy-start | bytes 6148
  283.0 4.2 copy-start
  283.0 5.0 copy-start.29
  283.0 10.8 %copy-start.21 = (f32[24,64,512]{2,1,0:T(8,128)S(1)}, f32[24,64,512]{2,1,0:T(8,128)}, u32[]{:S(2)}) copy-start(f32[24,64,512]{2,1,0:T(8,128)} %fusion.2) | copy-start | bytes 9437188
  287.2 6.6 copy-start.11
  287.2 6.6 copy-start.37
  287.2 6.6 copy-start.92
  300.5 11.2 %copy-start.42 = (f32[1792]{0:T(1024)S(1)}, f32[1792]{0:T(1024)}, u32[]{:S(2)}) copy-start(f32[1792]{0:T(1024)} %copy-done.41) | copy-start | bytes 21508
  300.5 11.2 %copy-start.44 = (f32[1792]{0:T(1024)S(1)}, f32[1792]{0:T(1024)}, u32[]{:S(2)}) copy-start(f32[1792]{0:T(1024)} %copy-done.43) | copy-start | bytes 21508
  313.3 4.7 copy-start.30
  313.4 4.7 copy-start.31
  313.4 4.7 copy-start.76
  313.4 4.7 copy-start.78
  313.4 4.7 copy-start.80
  313.4 4.7 copy-start.82
  313.4 6.0 copy-start.87
  316.4 13.7 %copy-start.38 = (f32[512,24]{0,1:T(8,128)S(1)}, f32[512,24]{0,1:T(8,128)}, u32[]{:S(2)}) copy-start(f32[512,24]{0,1:T(8,128)} %get-tuple-element.476) | copy-start | bytes 147460
  316.4 13.9 %copy-start.85 = (f32[24]{0:T(128)S(1)}, f32[24]{0:T(128)}, u32[]{:S(2)}) copy-start(f32[24]{0:T(128)} %copy-done.84) | copy-start | bytes 292
  316.5 15.9 %collective-permute-start.2 = (bf16[1,3,1792]{2,1,0:T(4,128)(2,1)S(1)}, bf16[1,3,1792]{2,1,0:T(4,128)(2,1)S(1)}, u32[]{:S(2)}, u32[]{:S(2)}) collective-permute-start(bf16[1,3,1792]{2,1,0:T(4,128)(2,1)S(1)} %slice.284), channel_id=1, source_target_pairs={{1,0},{2,1},{3,2},{5,4},{6,5},{7,6},{9,8},{10,9},{11,10},{13,12},{... | collective-permute-start | bytes 32264 | tf_op jit(solution)/shard_map/ppermute | solution.py:13
  330.3 4.6 copy-start.19
  330.3 4.6 copy-start.24
  330.4 4.6 copy-start.70
  330.4 4.6 copy-start.83
  332.4 5.7 copy-start.39
  332.4 5.7 slice-start
  359.1 353.9 %all-reduce.17.cloned.1.call-start = ((), (), s32[]{:S(2)}) async-start(), calls=%async_computation.5 | async-start | bytes 10010624 | tf_op jit(solution)/shard_map/psum | solution.py:241
  621.5 181.2 %all-gather.9.cloned.1.call-start = ((), (), s32[]{:S(2)}) async-start(), calls=%async_computation.2 | async-start | bytes 2949120 | tf_op jit(solution)/shard_map/all_gather | solution.py:254
  717.6 152.0 %all-gather.7.cloned.1.call-start = ((), (), s32[]{:S(2)}) async-start(), calls=%async_computation.1 | async-start | bytes 6635520 | tf_op jit(solution)/shard_map/all_gather | solution.py:253
  727.6 4.6 copy-start.8
  727.6 4.6 copy-start.49
  727.6 4.6 copy-start.66
  736.3 7.8 copy-start.73
  736.3 8.4 copy-start.71
  736.3 8.4 copy-start.86
  736.3 8.4 copy-start.88
  736.4 56.5 %copy-start.68 = (f32[512]{0:T(512)S(1)}, f32[512]{0:T(512)}, u32[]{:S(2)}) copy-start(f32[512]{0:T(512)} %copy-done.67) | copy-start | bytes 6148
  744.1 52.8 %copy-start.13 = (f32[192,3352]{0,1:T(8,128)S(1)}, f32[192,3352]{0,1:T(8,128)}, u32[]{:S(2)}) copy-start(f32[192,3352]{0,1:T(8,128)} %get-tuple-element.454) | copy-start | bytes 7723012
  (42 other events, 132.7 us)
Sparse Core Ops, SparseCore 0:
  58.8 36.3 all-gather.10
  169.0 70.9 all-gather.12
  359.2 256.4 reduce-scatter.3
  621.6 91.3 all-reduce.16
  717.7 52.3 all-gather.8
  771.5 98.0 all-gather.6
